TPU v7x, 32 devices: a whole 2x2x4 slice. The times are simulated.
32 devices in a mesh: fsdp: 8 (over z, x), dp: 4 (over y, core).
Axes of the slice: x: 2, y: 2, z: 4, core: 2. Of those that a mesh axis runs over, the one named last changes fastest.
Arguments:
- inputs: bfloat16 [18464, 1024], P(('fsdp', 'dp')), may hold values from -6 to 6
- cotangent: bfloat16 [18464, 1024], P(('fsdp', 'dp')), may hold values from -6 to 6
- norm1_gain: float32 [1024], P('fsdp'), may hold values from 0.08 to 2.5
- norm1_bias: float32 [1024], P('fsdp'), may hold values from -1.2 to 1.2
- qkv_weight: float32 [1024, 3072], P('fsdp'), may hold values from -0.1875 to 0.1875
- qv_bias: float32 [2048], P('fsdp'), may hold values from -3 to 3
- out_weight: float32 [1024, 1024], P('fsdp'), may hold values from -3 to 3
- out_bias: float32 [1024], P('fsdp'), may hold values from -3 to 3
- norm2_gain: float32 [1024], P('fsdp'), may hold values from 0.08 to 2.5
- norm2_bias: float32 [1024], P('fsdp'), may hold values from -1.2 to 1.2
- in_weight: float32 [1024, 4096], P('fsdp'), may hold values from -0.1875 to 0.1875
- in_bias: float32 [4096], P('fsdp'), may hold values from -3 to 3
- down_weight: float32 [4096, 1024], P('fsdp'), may hold values from -0.09375 to 0.09375
- down_bias: float32 [1024], P('fsdp'), may hold values from -3 to 3
- qkv_rows: float32 [1024], P('fsdp'), may hold values from 0.34375 to 196.875
- qkv_cols: float32 [3072], replicated, may hold values from 0.9375 to 93.75
- out_rows: float32 [1024], P('fsdp'), may hold values from 0.003125 to 2.8125
- out_cols: float32 [1024], replicated, may hold values from 0.009375 to 0.9375
- in_rows: float32 [1024], P('fsdp'), may hold values from 0.05625 to 31.5625
- in_cols: float32 [4096], replicated, may hold values from 0.15625 to 15.625
- down_rows: float32 [4096], P('fsdp'), may hold values from 0.20833333 to 187.5
- down_cols: float32 [1024], replicated, may hold values from 0.625 to 62.5
- norm1_gain_moment: float32 [1024], P('fsdp'), may hold values from 0.104166667 to 281.25
- norm1_bias_moment: float32 [1024], P('fsdp'), may hold values from 0.104166667 to 281.25
- qv_bias_moment: float32 [2048], P('fsdp'), may hold values from 0.104166667 to 281.25
- out_bias_moment: float32 [1024], P('fsdp'), may hold values from 0.104166667 to 281.25
- norm2_gain_moment: float32 [1024], P('fsdp'), may hold values from 0.104166667 to 281.25
- norm2_bias_moment: float32 [1024], P('fsdp'), may hold values from 0.104166667 to 281.25
- in_bias_moment: float32 [4096], P('fsdp'), may hold values from 0.104166667 to 281.25
- down_bias_moment: float32 [1024], P('fsdp'), may hold values from 0.104166667 to 281.25
Outputs:
- output: bfloat16 [18464, 1024], P(('fsdp', 'dp'))
- input_grad: bfloat16 [18464, 1024], P(('fsdp', 'dp'))
- grad_norm1_gain: float32 [1024], P('fsdp')
- grad_norm1_bias: float32 [1024], P('fsdp')
- grad_qkv_weight: float32 [1024, 3072], P('fsdp')
- grad_qv_bias: float32 [2048], P('fsdp')
- grad_out_weight: float32 [1024, 1024], P('fsdp')
- grad_out_bias: float32 [1024], P('fsdp')
- grad_norm2_gain: float32 [1024], P('fsdp')
- grad_norm2_bias: float32 [1024], P('fsdp')
- grad_in_weight: float32 [1024, 4096], P('fsdp')
- grad_in_bias: float32 [4096], P('fsdp')
- grad_down_weight: float32 [4096, 1024], P('fsdp')
- grad_down_bias: float32 [1024], P('fsdp')
- new_qkv_rows: float32 [1024], P('fsdp')
- new_qkv_cols: float32 [3072], replicated
- new_out_rows: float32 [1024], P('fsdp')
- new_out_cols: float32 [1024], replicated
- new_in_rows: float32 [1024], P('fsdp')
- new_in_cols: float32 [4096], replicated
- new_down_rows: float32 [4096], P('fsdp')
- new_down_cols: float32 [1024], replicated
- new_norm1_gain_moment: float32 [1024], P('fsdp')
- new_norm1_bias_moment: float32 [1024], P('fsdp')
- new_qv_bias_moment: float32 [2048], P('fsdp')
- new_out_bias_moment: float32 [1024], P('fsdp')
- new_norm2_gain_moment: float32 [1024], P('fsdp')
- new_norm2_bias_moment: float32 [1024], P('fsdp')
- new_in_bias_moment: float32 [4096], P('fsdp')
- new_down_bias_moment: float32 [1024], P('fsdp')
- new_norm1_gain: float32 [1024], P('fsdp')
- new_norm1_bias: float32 [1024], P('fsdp')
- new_qkv_weight: float32 [1024, 3072], P('fsdp')
- new_qv_bias: float32 [2048], P('fsdp')
- new_out_weight: float32 [1024, 1024], P('fsdp')
- new_out_bias: float32 [1024], P('fsdp')
- new_norm2_gain: float32 [1024], P('fsdp')
- new_norm2_bias: float32 [1024], P('fsdp')
- new_in_weight: float32 [1024, 4096], P('fsdp')
- new_in_bias: float32 [4096], P('fsdp')
- new_down_weight: float32 [4096, 1024], P('fsdp')
- new_down_bias: float32 [1024], P('fsdp')
- clip_factors: float32 [12], replicated
All inputs are finite; a program needn't handle non-finite values.
Results may differ from a plain program's by a relative error of at most 0.01.
The roundings to bfloat16 on the way count: a program that leaves them out, or rounds other values in their place, can miss the bound.
Values may be sent and summed in bfloat16 or wider, within the bound.
No kernel may reach another device: no remote copies, remote signals or barrier semaphores. Data moves between devices by JAX's collectives and lax.ppermute only.
A program may use at most 256 MiB of HBM per device.

v0:
```python
import math
import jax
import jax.numpy as jnp
from jax import lax
from jax.sharding import PartitionSpec as P

HEAD_DIM = 64
SEQ = 577
ln_eps = 1e-06
clip_level = 0.05
step_rate = 4.0


def norm_rows(values):
    centre = values - jnp.mean(values, axis=-1, keepdims=True)
    spread = jnp.mean(centre * centre, axis=-1, keepdims=True)
    return centre * lax.rsqrt(spread + ln_eps)


def norm_affine(values, gain_full, bias_full):
    return norm_rows(values) * gain_full + bias_full


def gelu_exact(values):
    return jax.nn.gelu(values, approximate=False)


def plain_dot(left, right):
    return jnp.dot(left, right, preferred_element_type=jnp.float32)


def lead_dot(left, right):
    return lax.dot_general(
        left, right, (((0,), (0,)), ((), ())), preferred_element_type=jnp.float32
    )


def tail_dot(left, right):
    return lax.dot_general(
        left, right, (((1,), (1,)), ((), ())), preferred_element_type=jnp.float32
    )


def split_heads(rows):
    return rows.reshape(rows.shape[0], rows.shape[1] // HEAD_DIM, HEAD_DIM)


def attend(block):
    query_rows, key_rows, value_rows = block
    length, width = query_rows.shape
    scale = 1.0 / math.sqrt(HEAD_DIM)
    scores = (
        jnp.einsum(
            "qhd,khd->hqk",
            split_heads(query_rows),
            split_heads(key_rows),
            preferred_element_type=jnp.float32,
        )
        * scale
    )
    highest = jnp.max(scores, axis=-1, keepdims=True)
    exponent = jnp.exp(scores - highest)
    summed = jnp.sum(exponent, axis=-1, keepdims=True)
    probs = exponent / summed
    mixed = jnp.einsum(
        "hqk,khd->qhd",
        probs.astype(jnp.bfloat16),
        split_heads(value_rows),
        preferred_element_type=jnp.float32,
    )
    logsum = (highest + jnp.log(summed))[..., 0]
    return (mixed.reshape(length, width).astype(jnp.bfloat16), logsum)


def attend_back(block):
    query_rows, key_rows, value_rows, logsum, grad_rows = block
    length, width = query_rows.shape
    scale = 1.0 / math.sqrt(HEAD_DIM)
    query_h = split_heads(query_rows)
    key_h = split_heads(key_rows)
    value_h = split_heads(value_rows)
    grad_h = split_heads(grad_rows)
    scores = jnp.einsum("qhd,khd->hqk", query_h, key_h, preferred_element_type=jnp.float32) * scale
    probs = jnp.exp(scores - logsum[..., None])
    grad_probs = jnp.einsum("qhd,khd->hqk", grad_h, value_h, preferred_element_type=jnp.float32)
    grad_value = jnp.einsum(
        "hqk,qhd->khd", probs.astype(jnp.bfloat16), grad_h, preferred_element_type=jnp.float32
    )
    inner = jnp.sum(probs * grad_probs, axis=-1, keepdims=True)
    grad_scores = (probs * (grad_probs - inner)).astype(jnp.bfloat16) * jnp.asarray(
        scale, jnp.bfloat16
    )
    grad_query = jnp.einsum("hqk,khd->qhd", grad_scores, key_h, preferred_element_type=jnp.float32)
    grad_key = jnp.einsum("hqk,qhd->khd", grad_scores, query_h, preferred_element_type=jnp.float32)
    joined = jnp.concatenate(
        [
            grad_query.reshape(length, width),
            grad_key.reshape(length, width),
            grad_value.reshape(length, width),
        ],
        axis=1,
    )
    return joined.astype(jnp.bfloat16)


def on_device(
    inputs,
    cotangent,
    norm1_gain,
    norm1_bias,
    qkv_weight,
    qv_bias,
    out_weight,
    out_bias,
    norm2_gain,
    norm2_bias,
    in_weight,
    in_bias,
    down_weight,
    down_bias,
    qkv_rows,
    qkv_cols,
    out_rows,
    out_cols,
    in_rows,
    in_cols,
    down_rows,
    down_cols,
    norm1_gain_moment,
    norm1_bias_moment,
    qv_bias_moment,
    out_bias_moment,
    norm2_gain_moment,
    norm2_bias_moment,
    in_bias_moment,
    down_bias_moment,
):
    masters = [
        norm1_gain,
        norm1_bias,
        qkv_weight,
        qv_bias,
        out_weight,
        out_bias,
        norm2_gain,
        norm2_bias,
        in_weight,
        in_bias,
        down_weight,
        down_bias,
    ]
    halves = [member.astype(jnp.bfloat16) for member in masters]
    gathered = (
        lax.all_gather(halves[0], "fsdp", axis=0, tiled=True),
        lax.all_gather(halves[1], "fsdp", axis=0, tiled=True),
        lax.all_gather(halves[2], "fsdp", axis=0, tiled=True),
        lax.all_gather(halves[3], "fsdp", axis=0, tiled=True),
        lax.all_gather(halves[4], "fsdp", axis=0, tiled=True),
        lax.all_gather(halves[5], "fsdp", axis=0, tiled=True),
        lax.all_gather(halves[6], "fsdp", axis=0, tiled=True),
        lax.all_gather(halves[7], "fsdp", axis=0, tiled=True),
        lax.all_gather(halves[8], "fsdp", axis=0, tiled=True),
        lax.all_gather(halves[9], "fsdp", axis=0, tiled=True),
        lax.all_gather(halves[10], "fsdp", axis=0, tiled=True),
        lax.all_gather(halves[11], "fsdp", axis=0, tiled=True),
    )
    (
        gain_one,
        bias_one,
        weight_qkv,
        bias_qv,
        weight_out,
        bias_out,
        gain_two,
        bias_two,
        weight_in,
        bias_in,
        weight_down,
        bias_down,
    ) = gathered
    tokens, width = inputs.shape
    images = tokens // SEQ
    rows_in = inputs.astype(jnp.float32)
    normed_f, pull_one = jax.vjp(
        norm_affine, rows_in, gain_one.astype(jnp.float32), bias_one.astype(jnp.float32)
    )
    normed = normed_f.astype(jnp.bfloat16)
    qkv = plain_dot(normed, weight_qkv)
    bias_pair = bias_qv.astype(jnp.float32)
    query = (qkv[:, :width] + bias_pair[:width]).astype(jnp.bfloat16)
    keys = qkv[:, width : 2 * width].astype(jnp.bfloat16)
    values = (qkv[:, 2 * width :] + bias_pair[width:]).astype(jnp.bfloat16)
    query_img = query.reshape(images, SEQ, width)
    keys_img = keys.reshape(images, SEQ, width)
    values_img = values.reshape(images, SEQ, width)
    attended_img, logsum = lax.map(attend, (query_img, keys_img, values_img))
    attended = attended_img.reshape(tokens, width)
    middle = rows_in + plain_dot(attended, weight_out) + bias_out.astype(jnp.float32)
    normed_mid_f, pull_two = jax.vjp(
        norm_affine, middle, gain_two.astype(jnp.float32), bias_two.astype(jnp.float32)
    )
    normed_mid = normed_mid_f.astype(jnp.bfloat16)
    preact = plain_dot(normed_mid, weight_in) + bias_in.astype(jnp.float32)
    hidden_f, pull_gelu = jax.vjp(gelu_exact, preact)
    hidden = hidden_f.astype(jnp.bfloat16)
    final = middle + plain_dot(hidden, weight_down) + bias_down.astype(jnp.float32)
    output = final.astype(jnp.bfloat16)
    grad_out_rows = cotangent.astype(jnp.float32)
    term_down_weight = lead_dot(hidden, cotangent)
    term_down_bias = jnp.sum(grad_out_rows, axis=0)
    grad_hidden = tail_dot(cotangent, weight_down)
    (grad_preact,) = pull_gelu(grad_hidden)
    grad_preact_low = grad_preact.astype(jnp.bfloat16)
    term_in_weight = lead_dot(normed_mid, grad_preact_low)
    term_in_bias = jnp.sum(grad_preact_low.astype(jnp.float32), axis=0)
    grad_normed_mid = tail_dot(grad_preact_low, weight_in)
    grad_mid_norm, term_gain_two, term_bias_two = pull_two(grad_normed_mid)
    grad_mid = grad_out_rows + grad_mid_norm
    grad_mid_low = grad_mid.astype(jnp.bfloat16)
    term_out_weight = lead_dot(attended, grad_mid_low)
    term_out_bias = jnp.sum(grad_mid_low.astype(jnp.float32), axis=0)
    grad_attended = tail_dot(grad_mid_low, weight_out).astype(jnp.bfloat16)
    grad_qkv_img = lax.map(
        attend_back,
        (query_img, keys_img, values_img, logsum, grad_attended.reshape(images, SEQ, width)),
    )
    grad_qkv = grad_qkv_img.reshape(tokens, 3 * width)
    term_qkv_weight = lead_dot(normed, grad_qkv)
    column_sums = jnp.sum(grad_qkv.astype(jnp.float32), axis=0)
    term_qv_bias = jnp.concatenate([column_sums[:width], column_sums[2 * width :]])
    grad_normed = tail_dot(grad_qkv, weight_qkv)
    grad_in_norm, term_gain_one, term_bias_one = pull_one(grad_normed)
    input_grad = (grad_mid + grad_in_norm).astype(jnp.bfloat16)
    terms = [
        term_gain_one,
        term_bias_one,
        term_qkv_weight,
        term_qv_bias,
        term_out_weight,
        term_out_bias,
        term_gain_two,
        term_bias_two,
        term_in_weight,
        term_in_bias,
        term_down_weight,
        term_down_bias,
    ]
    pieces = (
        lax.psum_scatter(terms[0], ("fsdp", "dp"), scatter_dimension=0, tiled=True),
        lax.psum_scatter(terms[1], ("fsdp", "dp"), scatter_dimension=0, tiled=True),
        lax.psum_scatter(terms[2], ("fsdp", "dp"), scatter_dimension=0, tiled=True),
        lax.psum_scatter(terms[3], ("fsdp", "dp"), scatter_dimension=0, tiled=True),
        lax.psum_scatter(terms[4], ("fsdp", "dp"), scatter_dimension=0, tiled=True),
        lax.psum_scatter(terms[5], ("fsdp", "dp"), scatter_dimension=0, tiled=True),
        lax.psum_scatter(terms[6], ("fsdp", "dp"), scatter_dimension=0, tiled=True),
        lax.psum_scatter(terms[7], ("fsdp", "dp"), scatter_dimension=0, tiled=True),
        lax.psum_scatter(terms[8], ("fsdp", "dp"), scatter_dimension=0, tiled=True),
        lax.psum_scatter(terms[9], ("fsdp", "dp"), scatter_dimension=0, tiled=True),
        lax.psum_scatter(terms[10], ("fsdp", "dp"), scatter_dimension=0, tiled=True),
        lax.psum_scatter(terms[11], ("fsdp", "dp"), scatter_dimension=0, tiled=True),
    )
    shards = (
        lax.all_gather(pieces[0], "dp", axis=0, tiled=True),
        lax.all_gather(pieces[1], "dp", axis=0, tiled=True),
        lax.all_gather(pieces[2], "dp", axis=0, tiled=True),
        lax.all_gather(pieces[3], "dp", axis=0, tiled=True),
        lax.all_gather(pieces[4], "dp", axis=0, tiled=True),
        lax.all_gather(pieces[5], "dp", axis=0, tiled=True),
        lax.all_gather(pieces[6], "dp", axis=0, tiled=True),
        lax.all_gather(pieces[7], "dp", axis=0, tiled=True),
        lax.all_gather(pieces[8], "dp", axis=0, tiled=True),
        lax.all_gather(pieces[9], "dp", axis=0, tiled=True),
        lax.all_gather(pieces[10], "dp", axis=0, tiled=True),
        lax.all_gather(pieces[11], "dp", axis=0, tiled=True),
    )
    group_size = lax.axis_size("fsdp")
    images_all = images * group_size * lax.axis_size("dp")
    grads = [member / images_all for member in shards]
    row_states = [qkv_rows, out_rows, in_rows, down_rows]
    col_states = [qkv_cols, out_cols, in_cols, down_cols]
    moments = [
        norm1_gain_moment,
        norm1_bias_moment,
        qv_bias_moment,
        out_bias_moment,
        norm2_gain_moment,
        norm2_bias_moment,
        in_bias_moment,
        down_bias_moment,
    ]
    matrix_slots = {2: 0, 4: 1, 8: 2, 10: 3}
    vector_slots = {0: 0, 1: 1, 3: 2, 5: 3, 6: 4, 7: 5, 9: 6, 11: 7}
    prepared = []
    packs = []
    for number in range(12):
        weight = masters[number]
        squared = grads[number] * grads[number]
        if number in matrix_slots:
            position = matrix_slots[number]
            new_rows = 0.5 * row_states[position] + 0.5 * jnp.mean(squared, axis=1)
            prepared.append(new_rows)
            packs.append(
                jnp.concatenate(
                    [
                        jnp.sum(squared, axis=0),
                        jnp.stack([jnp.sum(new_rows), jnp.sum(weight * weight)]),
                    ]
                )
            )
        else:
            position = vector_slots[number]
            prepared.append(0.5 * moments[position] + 0.5 * squared)
            packs.append(jnp.sum(weight * weight).reshape(1))
    totals = [lax.psum(packed, "fsdp") for packed in packs]
    directions = []
    counts = []
    weight_sums = []
    direction_sums = []
    new_cols_all = [None] * 4
    for number in range(12):
        weight = masters[number]
        grad = grads[number]
        if number in matrix_slots:
            position = matrix_slots[number]
            rows_total = weight.shape[0] * group_size
            new_cols = 0.5 * col_states[position] + 0.5 * totals[number][:-2] / rows_total
            new_cols_all[position] = new_cols
            mean_rows = totals[number][-2] / rows_total
            estimate = prepared[number][:, None] * new_cols[None, :] / mean_rows
            direction = grad * lax.rsqrt(estimate)
            counts.append(rows_total * weight.shape[1])
            weight_sums.append(totals[number][-1])
        else:
            direction = grad * lax.rsqrt(prepared[number])
            counts.append(weight.shape[0] * group_size)
            weight_sums.append(totals[number][0])
        directions.append(direction)
        direction_sums.append(jnp.sum(direction * direction))
    direction_totals = [lax.psum(value_sum, "fsdp") for value_sum in direction_sums]
    new_params = []
    clips = []
    for number in range(12):
        weight = masters[number]
        clip_factor = jnp.maximum(
            1.0, jnp.sqrt(direction_totals[number] / counts[number]) / clip_level
        )
        rms_weight = jnp.sqrt(weight_sums[number] / counts[number])
        new_params.append(weight - step_rate * rms_weight * directions[number] / clip_factor)
        clips.append(clip_factor)
    clip_factors = jnp.stack(clips)
    new_rows_all = [prepared[2], prepared[4], prepared[8], prepared[10]]
    new_moments = [
        prepared[0],
        prepared[1],
        prepared[3],
        prepared[5],
        prepared[6],
        prepared[7],
        prepared[9],
        prepared[11],
    ]
    return (
        output,
        input_grad,
        grads[0],
        grads[1],
        grads[2],
        grads[3],
        grads[4],
        grads[5],
        grads[6],
        grads[7],
        grads[8],
        grads[9],
        grads[10],
        grads[11],
        new_rows_all[0],
        new_cols_all[0],
        new_rows_all[1],
        new_cols_all[1],
        new_rows_all[2],
        new_cols_all[2],
        new_rows_all[3],
        new_cols_all[3],
        new_moments[0],
        new_moments[1],
        new_moments[2],
        new_moments[3],
        new_moments[4],
        new_moments[5],
        new_moments[6],
        new_moments[7],
        new_params[0],
        new_params[1],
        new_params[2],
        new_params[3],
        new_params[4],
        new_params[5],
        new_params[6],
        new_params[7],
        new_params[8],
        new_params[9],
        new_params[10],
        new_params[11],
        clip_factors,
    )


def solution(mesh):
    in_specs = (
        P(("fsdp", "dp"), None),
        P(("fsdp", "dp"), None),
        P("fsdp"),
        P("fsdp"),
        P("fsdp", None),
        P("fsdp"),
        P("fsdp", None),
        P("fsdp"),
        P("fsdp"),
        P("fsdp"),
        P("fsdp", None),
        P("fsdp"),
        P("fsdp", None),
        P("fsdp"),
        P("fsdp"),
        P(),
        P("fsdp"),
        P(),
        P("fsdp"),
        P(),
        P("fsdp"),
        P(),
        P("fsdp"),
        P("fsdp"),
        P("fsdp"),
        P("fsdp"),
        P("fsdp"),
        P("fsdp"),
        P("fsdp"),
        P("fsdp"),
    )
    out_specs = (
        P(("fsdp", "dp"), None),
        P(("fsdp", "dp"), None),
        P("fsdp"),
        P("fsdp"),
        P("fsdp", None),
        P("fsdp"),
        P("fsdp", None),
        P("fsdp"),
        P("fsdp"),
        P("fsdp"),
        P("fsdp", None),
        P("fsdp"),
        P("fsdp", None),
        P("fsdp"),
        P("fsdp"),
        P(),
        P("fsdp"),
        P(),
        P("fsdp"),
        P(),
        P("fsdp"),
        P(),
        P("fsdp"),
        P("fsdp"),
        P("fsdp"),
        P("fsdp"),
        P("fsdp"),
        P("fsdp"),
        P("fsdp"),
        P("fsdp"),
        P("fsdp"),
        P("fsdp"),
        P("fsdp", None),
        P("fsdp"),
        P("fsdp", None),
        P("fsdp"),
        P("fsdp"),
        P("fsdp"),
        P("fsdp", None),
        P("fsdp"),
        P("fsdp", None),
        P("fsdp"),
        P(),
    )
    return jax.shard_map(
        on_device, mesh=mesh, in_specs=in_specs, out_specs=out_specs, check_vma=False
    )
```

profile of v0, /device:TPU:0, one launch (start us, length us, event | category | flops | bytes accessed | tf_op | source)
XLA Modules:
  0.0 1457.1 jit_solution(12676742999869469270)
XLA Ops:
  7.3 3.8 multiply_reduce_fusion.14
  14.8 4.3 multiply_reduce_fusion.7
  21.2 22.4 %all-gather.5 = bf16[8,1,128]{2,1,0:T(2,128)(2,1)S(1)} all-gather(bf16[1,1,128]{2,1,0:T(2,128)(2,1)S(1)} %get-tuple-element.209), channel_id=1, replica_groups=mesh['fsdp'=8,'dp'=4] {'fsdp'}, dimensions={0}, use_global_device_ids=true | all-gather | bytes 2304 | tf_op jit(solution)/shard_map/all_gather | solution.py:161
  44.2 16.4 %all-gather.4 = bf16[8,1,128]{2,1,0:T(2,128)(2,1)S(1)} all-gather(bf16[1,1,128]{2,1,0:T(2,128)(2,1)S(1)} %get-tuple-element.211), channel_id=1, replica_groups=mesh['fsdp'=8,'dp'=4] {'fsdp'}, dimensions={0}, use_global_device_ids=true | all-gather | bytes 2304 | tf_op jit(solution)/shard_map/all_gather | solution.py:160
  61.2 18.2 %all-gather.3 = bf16[8,1,128]{2,1,0:T(2,128)(2,1)S(1)} all-gather(bf16[1,1,128]{2,1,0:T(2,128)(2,1)S(1)} %get-tuple-element.213), channel_id=1, replica_groups=mesh['fsdp'=8,'dp'=4] {'fsdp'}, dimensions={0}, use_global_device_ids=true | all-gather | bytes 2304 | tf_op jit(solution)/shard_map/all_gather | solution.py:159
  80.0 16.5 %all-gather.1 = bf16[8,1,128]{2,1,0:T(2,128)(2,1)S(1)} all-gather(bf16[1,1,128]{2,1,0:T(2,128)(2,1)S(1)} %get-tuple-element.215), channel_id=1, replica_groups=mesh['fsdp'=8,'dp'=4] {'fsdp'}, dimensions={0}, use_global_device_ids=true | all-gather | bytes 2304 | tf_op jit(solution)/shard_map/all_gather | solution.py:155
  97.2 18.0 %all-gather = bf16[8,1,128]{2,1,0:T(2,128)(2,1)S(1)} all-gather(bf16[1,1,128]{2,1,0:T(2,128)(2,1)S(1)} %get-tuple-element.217), channel_id=1, replica_groups=mesh['fsdp'=8,'dp'=4] {'fsdp'}, dimensions={0}, use_global_device_ids=true | all-gather | bytes 2304 | tf_op jit(solution)/shard_map/all_gather | solution.py:154
  115.2 26.1 %all-gather.6 = bf16[8,1,512]{2,1,0:T(2,128)(2,1)S(1)} all-gather(bf16[1,1,512]{2,1,0:T(2,128)(2,1)S(1)} %reshape.379), channel_id=1, replica_groups=mesh['fsdp'=8,'dp'=4] {'fsdp'}, dimensions={0}, use_global_device_ids=true | all-gather | bytes 9216 | tf_op jit(solution)/shard_map/all_gather | solution.py:163
  141.3 17.0 %all-gather.2 = bf16[8,1,256]{2,1,0:T(2,128)(2,1)S(1)} all-gather(bf16[1,1,256]{2,1,0:T(2,128)(2,1)S(1)} %reshape.371), channel_id=1, replica_groups=mesh['fsdp'=8,'dp'=4] {'fsdp'}, dimensions={0}, use_global_device_ids=true | all-gather | bytes 4608 | tf_op jit(solution)/shard_map/all_gather | solution.py:157
  159.1 6.6 fusion.80
  171.5 2.9 copy.93
  174.5 10.1 multiply_reduce_fusion.1
  184.6 10.6 fusion.2
  195.1 11.5 fusion.60
  206.6 3.9 fusion.100
  211.6 78.3 %all-gather.21.cloned.1.call-done = bf16[1024,4096]{1,0:T(8,128)(2,1)} async-done(((bf16[128,4096]{1,0:T(8,128)(2,1)}), bf16[1024,4096]{1,0:T(8,128)(2,1)}) %all-gather.21.cloned.1.call-update) | async-done | bytes 8388624 | tf_op jit(solution)/shard_map/all_gather | solution.py:162
  289.9 11.4 fusion.85
  301.3 114.3 %all-gather.23.cloned.1.call-done = bf16[4096,1024]{1,0:T(8,128)(2,1)} async-done(((bf16[512,1024]{1,0:T(8,128)(2,1)}), bf16[4096,1024]{1,0:T(8,128)(2,1)}) %all-gather.23.cloned.1.call-update) | async-done | bytes 8388624 | tf_op jit(solution)/shard_map/all_gather | solution.py:164
  415.6 30.8 %convert_reduce_fusion = (f32[4096]{0:T(1024)S(1)}, bf16[577,4096]{1,0:T(8,128)(2,1)S(1)}, f32[577,4096]{1,0:T(8,128)}) fusion(f32[577,4096]{1,0:T(8,128)} %fusion.85, f32[4096]{0:T(1024)S(1)} %bitcast.135, bf16[577,1024]{1,0:T(8,128)(2,1)} %param.31, bf16[4096,1024]{1,0:T(8,128)(2,1)} %all-gather.23.cloned.1.call-done), kind=kOutput, calls=%fused_computation.22 | convolution fusion | flops 5017477120 | bytes 33236992 | tf_op jit(solution)/shard_map/dot_general | solution.py:39
  446.4 5.6 multiply_reduce_fusion.2
  460.4 13.6 fusion.101
  474.0 13.4 fusion.57
  487.5 32.9 %fusion.47 = bf16[16,64,577]{2,1,0:T(8,128)(2,1)} fusion(bf16[577,16,64]{0,2,1:T(8,128)(2,1)} %bitcast.120, f32[16,577,577]{1,2,0:T(8,128)} %fusion.101, f32[16,577,577]{1,2,0:T(8,128)} %get-tuple-element.219, f32[16,577]{1,0:T(8,128)S(1)} %copy-done.23), kind=kOutput, calls=%fused_computation.85 | convolution fusion | flops 746361600 | bytes 45015232 | tf_op jit(solution)/shard_map/while/body/eval_jaxpr/hqk,khd->qhd/dot_general | solution.py:93
  520.4 33.3 %fusion.52 = bf16[16,64,577]{2,1,0:T(8,128)(2,1)} fusion(bf16[577,16,64]{0,2,1:T(8,128)(2,1)} %bitcast.118, f32[16,577,577]{1,2,0:T(8,128)} %fusion.101, f32[16,577,577]{1,2,0:T(8,128)} %get-tuple-element.219, f32[16,577]{1,0:T(8,128)S(1)} %copy-done.23), kind=kOutput, calls=%fused_computation.86 | convolution fusion | flops 746361600 | bytes 45015232 | tf_op jit(solution)/shard_map/while/body/eval_jaxpr/hqk,qhd->khd/dot_general | solution.py:94
  553.7 12.5 fusion.78
  566.8 13.0 fusion.84
  580.1 12.0 multiply_convert_fusion.1
  592.0 12.5 fusion.103
  604.6 5.6 fusion.102
  610.3 109.6 %reduce-scatter.5.cloned.1.call-done = f32[32,3072]{1,0:T(8,128)} async-done(((f32[1024,3072]{1,0:T(8,128)}), f32[32,3072]{1,0:T(8,128)}) %reduce-scatter.5.cloned.1.call-update) | async-done | bytes 393232 | tf_op jit(solution)/shard_map/reduce_scatter | solution.py:251
  725.3 179.0 %reduce-scatter.9.cloned.1.call-done = f32[32,4096]{1,0:T(8,128)} async-done(((f32[1024,4096]{1,0:T(8,128)}), f32[32,4096]{1,0:T(8,128)}) %reduce-scatter.9.cloned.1.call-update) | async-done | bytes 524304 | tf_op jit(solution)/shard_map/reduce_scatter | solution.py:257
  904.6 8.8 fusion.86
  918.0 48.0 %all-reduce.15 = (f32[1024]{0:T(1024)S(1)}, f32[1024]{0:T(1024)S(1)}, f32[2048]{0:T(1024)S(1)}, f32[1024]{0:T(1024)S(1)}, f32[1024]{0:T(1024)S(1)}, /*index=5*/f...) all-reduce(f32[1024]{0:T(1024)S(1)} %get-tuple-element.84, ...), channel_id=2, replica_groups=mesh['fsdp'=8,'dp'=4] {'fsdp','dp'}, use_global_device_ids=true, to_apply=%region_12.13.clone | all-reduce | flops 12288 | bytes 98304
  967.1 125.8 %reduce-scatter.11.cloned.1.call-done = f32[128,1024]{1,0:T(8,128)} async-done(((f32[4096,1024]{1,0:T(8,128)}), f32[128,1024]{1,0:T(8,128)}) %reduce-scatter.11.cloned.1.call-update) | async-done | bytes 524304 | tf_op jit(solution)/shard_map/reduce_scatter | solution.py:259
  1093.1 6.0 all-reduce.18
  1099.1 5.0 all-gather.8
  1107.9 130.0 %reduce-scatter.7.cloned.1.call-done = f32[32,1024]{1,0:T(8,128)} async-done(((f32[1024,1024]{1,0:T(8,128)}), f32[32,1024]{1,0:T(8,128)}) %reduce-scatter.7.cloned.1.call-update) | async-done | bytes 131088 | tf_op jit(solution)/shard_map/reduce_scatter | solution.py:253
  1237.9 6.7 all_gather.88
  1246.8 8.3 all-gather.25.cloned.1.call-done
  1259.8 19.3 %all-gather.27.cloned.1.call-done = f32[128,4096]{1,0:T(8,128)} async-done(((f32[32,4096]{1,0:T(8,128)}), f32[128,4096]{1,0:T(8,128)}) %all-gather.27.cloned.1.call-update) | async-done | bytes 2097168 | tf_op jit(solution)/shard_map/all_gather | solution.py:271
  1279.2 3.2 multiply_reduce_fusion.11
  1283.0 20.4 %all-gather.29.cloned.1.call-done = f32[512,1024]{1,0:T(8,128)} async-done(((f32[128,1024]{1,0:T(8,128)}), f32[512,1024]{1,0:T(8,128)}) %all-gather.29.cloned.1.call-update) | async-done | bytes 2097168 | tf_op jit(solution)/shard_map/all_gather | solution.py:273
  1303.4 3.3 multiply_reduce_fusion.9
  1309.9 37.9 %all-reduce.17 = (f32[3074]{0:T(1024)S(1)}, f32[1026]{0:T(1024)S(1)}, f32[4098]{0:T(1024)S(1)}, f32[1026]{0:T(1024)S(1)}) all-reduce(f32[3074]{0:T(1024)S(1)} %concatenate.22, f32[1026]{0:T(1024)S(1)} %concatenate.23, f32[4098]{0:T(1024)S(1)} %concatenate.24, f32[1026]{0:T(1024)S(1)} %concatenate.25), channel_id=1, replica_groups=mesh['fsdp'=8,'dp'=4] {'fsdp'}, use_global_device_ids=true, to_apply=%region_35.36 | all-reduce | flops 9224 | bytes 73792 | tf_op jit(solution)/shard_map/psum | solution.py:314
  1362.4 33.0 %all-reduce.16 = (f32[]{:T(128)}, f32[1]{0:T(128)}, f32[]{:T(128)}, f32[1]{0:T(128)}, f32[]{:T(128)}, /*index=5*/f32[]{:T(128)}, f32[1]{0:T(128)}, f32[]{:T(128)...) all-reduce(f32[]{:T(128)} %get-tuple-element.230, ...), channel_id=1, replica_groups=mesh['fsdp'=8,'dp'=4] {'fsdp'}, use_global_device_ids=true, to_apply=%region_54.55 | all-reduce | flops 20 | bytes 160 | tf_op jit(solution)/shard_map/psum | solution.py:339
  1410.5 16.5 %all-gather.7 = bf16[8,1,128]{2,1,0:T(2,128)(2,1)S(1)} all-gather(bf16[1,1,128]{2,1,0:T(2,128)(2,1)S(1)} %get-tuple-element.207), channel_id=1, replica_groups=mesh['fsdp'=8,'dp'=4] {'fsdp'}, dimensions={0}, use_global_device_ids=true | all-gather | bytes 2304 | tf_op jit(solution)/shard_map/all_gather | solution.py:165
  1428.0 3.1 divide_subtract_fusion.2
  1440.5 9.7 add_convert_fusion.2
  (306 shorter events, 70.3 us)
Async XLA Ops:
  7.3 151.8 %all-gather.17.cloned.1.call-start = ((), (), s32[]{:S(2)}) async-start(), calls=%async_computation.4 | async-start | bytes 7077888 | tf_op jit(solution)/shard_map/all_gather | solution.py:156
  11.2 195.5 %all-gather.19.cloned.1.call-start = ((), (), s32[]{:S(2)}) async-start(), calls=%async_computation.5 | async-start | bytes 2359296 | tf_op jit(solution)/shard_map/all_gather | solution.py:158
  12.6 277.3 %all-gather.21.cloned.1.call-start = ((), (), s32[]{:S(2)}) async-start(), calls=%async_computation.6 | async-start | bytes 9437184 | tf_op jit(solution)/shard_map/all_gather | solution.py:162
  14.8 81.8 %copy-start.79 = (f32[128]{0:T(128)S(1)}, f32[128]{0:T(128)}, u32[]{:S(2)}) copy-start(f32[128]{0:T(128)} %param.32) | copy-start | bytes 1540
  14.8 143.5 %copy-start.2 = (bf16[577,1024]{1,0:T(8,128)(2,1)S(1)}, bf16[577,1024]{1,0:T(8,128)(2,1)}, u32[]{:S(2)}) copy-start(bf16[577,1024]{1,0:T(8,128)(2,1)} %param.30) | copy-start | bytes 3545092
  14.8 400.8 %all-gather.23.cloned.1.call-start = ((), (), s32[]{:S(2)}) async-start(), calls=%async_computation.7 | async-start | bytes 9437184 | tf_op jit(solution)/shard_map/all_gather | solution.py:164
  19.2 700.7 %reduce-scatter.5.cloned.1.call-start = ((), (), s32[]{:S(2)}) async-start(), calls=%async_computation.8 | async-start | bytes 12976128 | tf_op jit(solution)/shard_map/reduce_scatter | solution.py:251
  43.6 246.3 %copy-start.21 = (f32[8,1,128]{2,1,0:T(1,128)}, f32[8,1,128]{2,1,0:T(1,128)S(1)}, u32[]{:S(2)}) copy-start(f32[8,1,128]{2,1,0:T(1,128)S(1)} %convert_element_type.176) | copy-start | bytes 12292
  566.2 338.1 %reduce-scatter.9.cloned.1.call-start = ((), (), s32[]{:S(2)}) async-start(), calls=%async_computation.11 | async-start | bytes 17301504 | tf_op jit(solution)/shard_map/reduce_scatter | solution.py:257
  579.8 513.0 %reduce-scatter.11.cloned.1.call-start = ((), (), s32[]{:S(2)}) async-start(), calls=%async_computation.13 | async-start | bytes 17301504 | tf_op jit(solution)/shard_map/reduce_scatter | solution.py:259
  604.6 633.3 %reduce-scatter.7.cloned.1.call-start = ((), (), s32[]{:S(2)}) async-start(), calls=%async_computation.10 | async-start | bytes 4325376 | tf_op jit(solution)/shard_map/reduce_scatter | solution.py:253
  610.2 109.8 %copy-start.91 = (u32[32]{0:T(128)S(1)}, u32[32]{0:T(128)}, u32[]{:S(2)}) copy-start(u32[32]{0:T(128)} %constant.266) | copy-start | bytes 388
  610.2 111.6 %copy-start.75 = (f32[128]{0:T(128)S(1)}, f32[128]{0:T(128)}, u32[]{:S(2)}) copy-start(f32[128]{0:T(128)} %param.43) | copy-start | bytes 1540
  610.2 644.8 %all-gather.25.cloned.1.call-start = ((), (), s32[]{:S(2)}) async-start(), calls=%async_computation.9 | async-start | bytes 1966080 | tf_op jit(solution)/shard_map/all_gather | solution.py:265
  719.9 559.3 %all-gather.27.cloned.1.call-start = ((), (), s32[]{:S(2)}) async-start(), calls=%async_computation.12 | async-start | bytes 2621440 | tf_op jit(solution)/shard_map/all_gather | solution.py:271
  904.3 399.1 %all-gather.29.cloned.1.call-start = ((), (), s32[]{:S(2)}) async-start(), calls=%async_computation.14 | async-start | bytes 2621440 | tf_op jit(solution)/shard_map/all_gather | solution.py:273
  915.7 188.4 %copy-start.68 = (f32[256]{0:T(256)S(1)}, f32[256]{0:T(256)}, u32[]{:S(2)}) copy-start(f32[256]{0:T(256)} %param.54) | copy-start | bytes 3076
  915.7 189.0 %copy-start.69 = (f32[128]{0:T(128)S(1)}, f32[128]{0:T(128)}, u32[]{:S(2)}) copy-start(f32[128]{0:T(128)} %param.53) | copy-start | bytes 1540
  915.7 189.0 %copy-start.70 = (f32[128]{0:T(128)S(1)}, f32[128]{0:T(128)}, u32[]{:S(2)}) copy-start(f32[128]{0:T(128)} %param.52) | copy-start | bytes 1540
  915.7 189.6 %copy-start.71 = (f32[128]{0:T(128)S(1)}, f32[128]{0:T(128)}, u32[]{:S(2)}) copy-start(f32[128]{0:T(128)} %param.56) | copy-start | bytes 1540
  915.8 189.6 %copy-start.72 = (f32[128]{0:T(128)S(1)}, f32[128]{0:T(128)}, u32[]{:S(2)}) copy-start(f32[128]{0:T(128)} %param.55) | copy-start | bytes 1540
  915.8 190.3 %copy-start.73 = (f32[128]{0:T(128)S(1)}, f32[128]{0:T(128)}, u32[]{:S(2)}) copy-start(f32[128]{0:T(128)} %param.59) | copy-start | bytes 1540
  915.8 190.3 %copy-start.74 = (f32[128]{0:T(128)S(1)}, f32[128]{0:T(128)}, u32[]{:S(2)}) copy-start(f32[128]{0:T(128)} %param.57) | copy-start | bytes 1540
  915.8 191.5 %copy-start.56 = (f32[512]{0:T(512)S(1)}, f32[512]{0:T(512)}, u32[]{:S(2)}) copy-start(f32[512]{0:T(512)} %param.58) | copy-start | bytes 6148
  918.0 326.7 %copy-start.76 = (f32[128]{0:T(128)S(1)}, f32[128]{0:T(128)}, u32[]{:S(2)}) copy-start(f32[128]{0:T(128)} %param.46) | copy-start | bytes 1540
  1104.1 332.0 %copy-start.37 = (f32[4,1,128]{2,1,0:T(1,128)}, f32[4,1,128]{2,1,0:T(1,128)S(1)}, u32[]{:S(2)}) copy-start(f32[4,1,128]{2,1,0:T(1,128)S(1)} %broadcast_multiply_fusion.6) | copy-start | bytes 6148
  1104.7 334.6 %copy-start.50 = (f32[256]{0:T(256)}, f32[256]{0:T(256)S(1)}, u32[]{:S(2)}) copy-start(f32[256]{0:T(256)S(1)} %get-tuple-element.151) | copy-start | bytes 3076
  1104.7 334.6 %copy-start.51 = (f32[256]{0:T(256)}, f32[256]{0:T(256)S(1)}, u32[]{:S(2)}) copy-start(f32[256]{0:T(256)S(1)} %get-tuple-element.152) | copy-start | bytes 3076
  1105.4 331.3 %copy-start.60 = (f32[128]{0:T(128)}, f32[128]{0:T(128)S(1)}, u32[]{:S(2)}) copy-start(f32[128]{0:T(128)S(1)} %get-tuple-element.231) | copy-start | bytes 1540
  1105.4 331.3 %copy-start.61 = (f32[128]{0:T(128)}, f32[128]{0:T(128)S(1)}, u32[]{:S(2)}) copy-start(f32[128]{0:T(128)S(1)} %get-tuple-element.232) | copy-start | bytes 1540
  1105.4 331.8 %copy-start.58 = (f32[128]{0:T(128)}, f32[128]{0:T(128)S(1)}, u32[]{:S(2)}) copy-start(f32[128]{0:T(128)S(1)} %get-tuple-element.154) | copy-start | bytes 1540
  1105.4 331.9 %copy-start.59 = (f32[128]{0:T(128)}, f32[128]{0:T(128)S(1)}, u32[]{:S(2)}) copy-start(f32[128]{0:T(128)S(1)} %get-tuple-element.155) | copy-start | bytes 1540
  1106.0 331.7 %copy-start.64 = (f32[128]{0:T(128)}, f32[128]{0:T(128)S(1)}, u32[]{:S(2)}) copy-start(f32[128]{0:T(128)S(1)} %get-tuple-element.228) | copy-start | bytes 1540
  1106.0 331.7 %copy-start.65 = (f32[128]{0:T(128)}, f32[128]{0:T(128)S(1)}, u32[]{:S(2)}) copy-start(f32[128]{0:T(128)S(1)} %get-tuple-element.229) | copy-start | bytes 1540
  1106.0 332.2 %copy-start.62 = (f32[128]{0:T(128)}, f32[128]{0:T(128)S(1)}, u32[]{:S(2)}) copy-start(f32[128]{0:T(128)S(1)} %get-tuple-element.145) | copy-start | bytes 1540
  1106.0 332.3 %copy-start.63 = (f32[128]{0:T(128)}, f32[128]{0:T(128)S(1)}, u32[]{:S(2)}) copy-start(f32[128]{0:T(128)S(1)} %get-tuple-element.146) | copy-start | bytes 1540
  1107.2 301.9 %copy-start.54 = (f32[128]{0:T(128)}, f32[128]{0:T(128)S(1)}, u32[]{:S(2)}) copy-start(f32[128]{0:T(128)S(1)} %get-tuple-element.137) | copy-start | bytes 1540
  1107.2 301.9 %copy-start.55 = (f32[128]{0:T(128)}, f32[128]{0:T(128)S(1)}, u32[]{:S(2)}) copy-start(f32[128]{0:T(128)S(1)} %get-tuple-element.138) | copy-start | bytes 1540
  1107.9 328.2 %copy-start.42 = (f32[512]{0:T(512)}, f32[512]{0:T(512)S(1)}, u32[]{:S(2)}) copy-start(f32[512]{0:T(512)S(1)} %get-tuple-element.140) | copy-start | bytes 6148
  1107.9 150.0 %copy-start.77 = (f32[128]{0:T(128)S(1)}, f32[128]{0:T(128)}, u32[]{:S(2)}) copy-start(f32[128]{0:T(128)} %param.44) | copy-start | bytes 1540
  1244.7 182.2 %copy-start.17 = (f32[128,1024]{1,0:T(8,128)}, f32[128,1024]{1,0:T(8,128)S(1)}, u32[]{:S(2)}) copy-start(f32[128,1024]{1,0:T(8,128)S(1)} %get-tuple-element.167) | copy-start | bytes 1572868
  1245.4 181.6 %copy-start.44 = (f32[128]{0:T(128)}, f32[128]{0:T(128)S(1)}, u32[]{:S(2)}) copy-start(f32[128]{0:T(128)S(1)} %get-tuple-element.166) | copy-start | bytes 1540
  1258.5 169.5 %copy-start.43 = (f32[128]{0:T(128)}, f32[128]{0:T(128)S(1)}, u32[]{:S(2)}) copy-start(f32[128]{0:T(128)S(1)} %get-tuple-element.169) | copy-start | bytes 1540
  1283.0 148.1 %copy-start.45 = (f32[128]{0:T(128)}, f32[128]{0:T(128)S(1)}, u32[]{:S(2)}) copy-start(f32[128]{0:T(128)S(1)} %get-tuple-element.163) | copy-start | bytes 1540
  1307.3 125.8 %copy-start.36 = (f32[512]{0:T(512)}, f32[512]{0:T(512)S(1)}, u32[]{:S(2)}) copy-start(f32[512]{0:T(512)S(1)} %get-tuple-element.160) | copy-start | bytes 6148
  1351.2 76.8 %copy-start.25 = (f32[3072]{0:T(1024)}, f32[3072]{0:T(1024)S(1)}, u32[]{:S(2)}) copy-start(f32[3072]{0:T(1024)S(1)} %fusion.63) | copy-start | bytes 36868
  1351.2 79.9 %copy-start.24 = (f32[4096]{0:T(1024)}, f32[4096]{0:T(1024)S(1)}, u32[]{:S(2)}) copy-start(f32[4096]{0:T(1024)S(1)} %fusion.62) | copy-start | bytes 49156
  1354.5 78.5 %copy-start.35 = (f32[1024]{0:T(1024)}, f32[1024]{0:T(1024)S(1)}, u32[]{:S(2)}) copy-start(f32[1024]{0:T(1024)S(1)} %get-tuple-element.233) | copy-start | bytes 12292
  (55 other events, 1095.6 us)
Sparse Core Ops, SparseCore 0:
  11.3 101.9 all-gather.16
  116.0 47.6 all-gather.18
  166.4 123.4 all-gather.20
  292.4 123.1 all-gather.22
  566.3 153.5 reduce-scatter.4
  722.1 182.1 reduce-scatter.8
  906.7 186.1 reduce-scatter.10
  1095.2 142.5 reduce-scatter.6
  1239.5 15.5 all-gather.24
  1256.5 22.5 all-gather.26
  1280.8 22.5 all-gather.28
where the time goes:
time: 1460 us
  waiting for transfers between devices  785 us (54%)
  blocking collectives  288 us (20%)
  matrix products  238 us (16%)
  other arithmetic  86.3 us (6%)
  between operations  35.5 us (2%)
  local copies, waits for them, and re-layouts  23.8 us (2%)
    reduce_scatter x1, waiting for transfers between devices, on_device(): lax.psum_scatter(terms[8], ('fsdp', 'dp'), scatter_dimension=0, tiled=True)  179 us
    reduce_scatter x1, waiting for transfers between devices, on_device(): lax.psum_scatter(terms[4], ('fsdp', 'dp'), scatter_dimension=0, tiled=True)  130 us
    reduce_scatter x1, waiting for transfers between devices, on_device(): lax.psum_scatter(terms[10], ('fsdp', 'dp'), scatter_dimension=0, tiled=True)  126 us
    all_gather x1, waiting for transfers between devices, on_device(): lax.all_gather(halves[10], 'fsdp', axis=0, tiled=True)  114 us
    reduce_scatter x1, waiting for transfers between devices, on_device(): lax.psum_scatter(terms[2], ('fsdp', 'dp'), scatter_dimension=0, tiled=True)  110 us
    all_gather x1, waiting for transfers between devices, on_device(): lax.all_gather(halves[8], 'fsdp', axis=0, tiled=True)  78.3 us
    unnamed x2, blocking collectives  54.1 us
    dot_general x4, matrix products, tail_dot(): lax.dot_general(left, right, (((1,), (1,)), ((), ())), preferred_element_...  47.7 us
  transfers between devices with their start and end apart: 11, of which 9 were waited for; matrix products, arithmetic and copies ran while one was open for 10% of the time, Pallas kernels for 0%

commit v1 on v0

--- a/solution.py
+++ b/solution.py
@@ -311,7 +311,7 @@
             position = vector_slots[number]
             prepared.append(0.5 * moments[position] + 0.5 * squared)
             packs.append(jnp.sum(weight * weight).reshape(1))
-    totals = [lax.psum(packed, "fsdp") for packed in packs]
+    totals = [jnp.sum(lax.all_gather(packed, "fsdp"), axis=0) for packed in packs]
     directions = []
     counts = []
     weight_sums = []

time: 1460 us -> 1580 us (1.082)
  waiting for transfers between devices: 785 us -> 895 us
  blocking collectives: 288 us -> 251 us
  local copies, waits for them, and re-layouts: 23.8 us -> 46 us
    unnamed x11 -> x15, waiting for transfers between devices: 0.18 us -> 133 us
    reduce_scatter x1, waiting for transfers between devices: 179 us -> 126 us  [on_device(): lax.psum_scatter(terms[8], ('fsdp', 'dp'), scatter_dimension=0, tiled=True)]
    reduce_scatter x1, waiting for transfers between devices: 126 us -> 165 us  [on_device(): lax.psum_scatter(terms[10], ('fsdp', 'dp'), scatter_dimension=0, tiled=True)]
    psum x1 -> x0, blocking collectives: 37.9 us -> none  [on_device(): totals = [lax.psum(packed, 'fsdp') for packed in packs]]
  transfers between devices with their start and end apart: 11 -> 13, of which waited for: 9 -> 11; matrix products, arithmetic and copies ran while one was open for 10% -> 12% of each run, Pallas kernels for 0% -> 0%
where the time goes in v1:
time: 1580 us; the launch traced here: 1570 us
  waiting for transfers between devices  895 us (57%)
  blocking collectives  251 us (16%)
  matrix products  242 us (15%)
  other arithmetic  99.3 us (6%)
  local copies, waits for them, and re-layouts  46 us (3%)
  between operations  37.7 us (2%)
    reduce_scatter x1, waiting for transfers between devices, on_device(): lax.psum_scatter(terms[10], ('fsdp', 'dp'), scatter_dimension=0, tiled=True)  165 us
    unnamed x15, waiting for transfers between devices  133 us
    reduce_scatter x1, waiting for transfers between devices, on_device(): lax.psum_scatter(terms[4], ('fsdp', 'dp'), scatter_dimension=0, tiled=True)  129 us
    reduce_scatter x1, waiting for transfers between devices, on_device(): lax.psum_scatter(terms[8], ('fsdp', 'dp'), scatter_dimension=0, tiled=True)  126 us
    all_gather x1, waiting for transfers between devices, on_device(): lax.all_gather(halves[10], 'fsdp', axis=0, tiled=True)  114 us
    reduce_scatter x1, waiting for transfers between devices, on_device(): lax.psum_scatter(terms[2], ('fsdp', 'dp'), scatter_dimension=0, tiled=True)  110 us
    all_gather x1, waiting for transfers between devices, on_device(): lax.all_gather(halves[8], 'fsdp', axis=0, tiled=True)  73.8 us
    unnamed x2, blocking collectives  53.8 us
  transfers between devices with their start and end apart: 13, of which 11 were waited for; matrix products, arithmetic and copies ran while one was open for 12% of the time, Pallas kernels for 0%

profile of v1, /device:TPU:0, one launch (start us, length us, event | category | flops | bytes accessed | tf_op | source)
XLA Modules:
  0.0 1572.1 jit_solution(8302127363680468905)
XLA Ops:
  7.3 3.8 multiply_reduce_fusion.14
  14.8 4.4 multiply_reduce_fusion.7
  21.1 22.4 %all-gather.9 = bf16[8,1,128]{2,1,0:T(2,128)(2,1)S(1)} all-gather(bf16[1,1,128]{2,1,0:T(2,128)(2,1)S(1)} %get-tuple-element.209), channel_id=1, replica_groups=mesh['fsdp'=8,'dp'=4] {'fsdp'}, dimensions={0}, use_global_device_ids=true | all-gather | bytes 2304 | tf_op jit(solution)/shard_map/all_gather | solution.py:161
  44.2 16.4 %all-gather.8 = bf16[8,1,128]{2,1,0:T(2,128)(2,1)S(1)} all-gather(bf16[1,1,128]{2,1,0:T(2,128)(2,1)S(1)} %get-tuple-element.211), channel_id=1, replica_groups=mesh['fsdp'=8,'dp'=4] {'fsdp'}, dimensions={0}, use_global_device_ids=true | all-gather | bytes 2304 | tf_op jit(solution)/shard_map/all_gather | solution.py:160
  61.1 18.2 %all-gather.7 = bf16[8,1,128]{2,1,0:T(2,128)(2,1)S(1)} all-gather(bf16[1,1,128]{2,1,0:T(2,128)(2,1)S(1)} %get-tuple-element.213), channel_id=1, replica_groups=mesh['fsdp'=8,'dp'=4] {'fsdp'}, dimensions={0}, use_global_device_ids=true | all-gather | bytes 2304 | tf_op jit(solution)/shard_map/all_gather | solution.py:159
  80.0 16.5 %all-gather.5 = bf16[8,1,128]{2,1,0:T(2,128)(2,1)S(1)} all-gather(bf16[1,1,128]{2,1,0:T(2,128)(2,1)S(1)} %get-tuple-element.215), channel_id=1, replica_groups=mesh['fsdp'=8,'dp'=4] {'fsdp'}, dimensions={0}, use_global_device_ids=true | all-gather | bytes 2304 | tf_op jit(solution)/shard_map/all_gather | solution.py:155
  97.1 18.0 %all-gather.4 = bf16[8,1,128]{2,1,0:T(2,128)(2,1)S(1)} all-gather(bf16[1,1,128]{2,1,0:T(2,128)(2,1)S(1)} %get-tuple-element.217), channel_id=1, replica_groups=mesh['fsdp'=8,'dp'=4] {'fsdp'}, dimensions={0}, use_global_device_ids=true | all-gather | bytes 2304 | tf_op jit(solution)/shard_map/all_gather | solution.py:154
  115.1 26.1 %all-gather.10 = bf16[8,1,512]{2,1,0:T(2,128)(2,1)S(1)} all-gather(bf16[1,1,512]{2,1,0:T(2,128)(2,1)S(1)} %reshape.363), channel_id=1, replica_groups=mesh['fsdp'=8,'dp'=4] {'fsdp'}, dimensions={0}, use_global_device_ids=true | all-gather | bytes 9216 | tf_op jit(solution)/shard_map/all_gather | solution.py:163
  141.2 16.4 %all-gather.6 = bf16[8,1,256]{2,1,0:T(2,128)(2,1)S(1)} all-gather(bf16[1,1,256]{2,1,0:T(2,128)(2,1)S(1)} %reshape.355), channel_id=1, replica_groups=mesh['fsdp'=8,'dp'=4] {'fsdp'}, dimensions={0}, use_global_device_ids=true | all-gather | bytes 4608 | tf_op jit(solution)/shard_map/all_gather | solution.py:157
  158.5 7.1 fusion.80
  176.0 13.3 multiply_reduce_fusion.1
  189.2 10.5 fusion.2
  199.8 11.4 fusion.60
  211.2 3.9 fusion.100
  216.1 73.8 %all-gather.25.cloned.1.call-done = bf16[1024,4096]{1,0:T(8,128)(2,1)} async-done(((bf16[128,4096]{1,0:T(8,128)(2,1)}), bf16[1024,4096]{1,0:T(8,128)(2,1)}) %all-gather.25.cloned.1.call-update) | async-done | bytes 8388624 | tf_op jit(solution)/shard_map/all_gather | solution.py:162
  289.9 11.4 fusion.85
  301.3 114.2 %all-gather.27.cloned.1.call-done = bf16[4096,1024]{1,0:T(8,128)(2,1)} async-done(((bf16[512,1024]{1,0:T(8,128)(2,1)}), bf16[4096,1024]{1,0:T(8,128)(2,1)}) %all-gather.27.cloned.1.call-update) | async-done | bytes 8388624 | tf_op jit(solution)/shard_map/all_gather | solution.py:164
  415.6 30.8 %convert_reduce_fusion = (f32[4096]{0:T(1024)S(1)}, bf16[577,4096]{1,0:T(8,128)(2,1)S(1)}, f32[577,4096]{1,0:T(8,128)}) fusion(f32[577,4096]{1,0:T(8,128)} %fusion.85, f32[4096]{0:T(1024)S(1)} %bitcast.131, bf16[577,1024]{1,0:T(8,128)(2,1)} %param.31, bf16[4096,1024]{1,0:T(8,128)(2,1)} %all-gather.27.cloned.1.call-done), kind=kOutput, calls=%fused_computation.22 | convolution fusion | flops 5017477120 | bytes 33236992 | tf_op jit(solution)/shard_map/dot_general | solution.py:39
  446.4 5.6 multiply_reduce_fusion.2
  460.5 13.6 fusion.101
  474.1 13.4 fusion.57
  487.5 32.9 %fusion.47 = bf16[16,64,577]{2,1,0:T(8,128)(2,1)} fusion(bf16[577,16,64]{0,2,1:T(8,128)(2,1)} %bitcast.116, f32[16,577,577]{1,2,0:T(8,128)} %fusion.101, f32[16,577,577]{1,2,0:T(8,128)} %get-tuple-element.219, f32[16,577]{1,0:T(8,128)S(1)} %copy-done.23), kind=kOutput, calls=%fused_computation.85 | convolution fusion | flops 746361600 | bytes 45015232 | tf_op jit(solution)/shard_map/while/body/eval_jaxpr/hqk,khd->qhd/dot_general | solution.py:93
  520.4 33.3 %fusion.52 = bf16[16,64,577]{2,1,0:T(8,128)(2,1)} fusion(bf16[577,16,64]{0,2,1:T(8,128)(2,1)} %bitcast.114, f32[16,577,577]{1,2,0:T(8,128)} %fusion.101, f32[16,577,577]{1,2,0:T(8,128)} %get-tuple-element.219, f32[16,577]{1,0:T(8,128)S(1)} %copy-done.23), kind=kOutput, calls=%fused_computation.86 | convolution fusion | flops 746361600 | bytes 45015232 | tf_op jit(solution)/shard_map/while/body/eval_jaxpr/hqk,qhd->khd/dot_general | solution.py:94
  553.7 12.5 fusion.78
  566.3 11.5 multiply_convert_fusion.1
  577.8 12.7 fusion.103
  591.2 13.3 fusion.84
  604.5 5.5 fusion.102
  610.1 109.8 %reduce-scatter.5.cloned.1.call-done = f32[32,3072]{1,0:T(8,128)} async-done(((f32[1024,3072]{1,0:T(8,128)}), f32[32,3072]{1,0:T(8,128)}) %reduce-scatter.5.cloned.1.call-update) | async-done | bytes 393232 | tf_op jit(solution)/shard_map/reduce_scatter | solution.py:251
  739.3 165.1 %reduce-scatter.11.cloned.1.call-done = f32[128,1024]{1,0:T(8,128)} async-done(((f32[4096,1024]{1,0:T(8,128)}), f32[128,1024]{1,0:T(8,128)}) %reduce-scatter.11.cloned.1.call-update) | async-done | bytes 524304 | tf_op jit(solution)/shard_map/reduce_scatter | solution.py:259
  904.7 8.8 fusion.86
  918.0 48.1 %all-reduce.27 = (f32[1024]{0:T(1024)S(1)}, f32[1024]{0:T(1024)S(1)}, f32[2048]{0:T(1024)S(1)}, f32[1024]{0:T(1024)S(1)}, f32[1024]{0:T(1024)S(1)}, /*index=5*/f...) all-reduce(f32[1024]{0:T(1024)S(1)} %get-tuple-element.84, ...), channel_id=6, replica_groups=mesh['fsdp'=8,'dp'=4] {'fsdp','dp'}, use_global_device_ids=true, to_apply=%region_12.13.clone | all-reduce | flops 12288 | bytes 98304
  967.2 126.2 %reduce-scatter.9.cloned.1.call-done = f32[32,4096]{1,0:T(8,128)} async-done(((f32[1024,4096]{1,0:T(8,128)}), f32[32,4096]{1,0:T(8,128)}) %reduce-scatter.9.cloned.1.call-update) | async-done | bytes 524304 | tf_op jit(solution)/shard_map/reduce_scatter | solution.py:257
  1093.6 5.7 all-reduce.31
  1099.4 5.0 all-gather.12
  1110.3 128.5 %reduce-scatter.7.cloned.1.call-done = f32[32,1024]{1,0:T(8,128)} async-done(((f32[1024,1024]{1,0:T(8,128)}), f32[32,1024]{1,0:T(8,128)}) %reduce-scatter.7.cloned.1.call-update) | async-done | bytes 131088 | tf_op jit(solution)/shard_map/reduce_scatter | solution.py:253
  1238.8 6.7 all_gather.136
  1248.0 8.0 all-gather.29.cloned.1.call-done
  1261.7 18.4 %all-gather.33.cloned.1.call-done = f32[512,1024]{1,0:T(8,128)} async-done(((f32[128,1024]{1,0:T(8,128)}), f32[512,1024]{1,0:T(8,128)}) %all-gather.33.cloned.1.call-update) | async-done | bytes 2097168 | tf_op jit(solution)/shard_map/all_gather | solution.py:273
  1280.1 3.3 multiply_reduce_fusion.9
  1286.6 17.8 %all-gather.31.cloned.1.call-done = f32[128,4096]{1,0:T(8,128)} async-done(((f32[32,4096]{1,0:T(8,128)}), f32[128,4096]{1,0:T(8,128)}) %all-gather.31.cloned.1.call-update) | async-done | bytes 2097168 | tf_op jit(solution)/shard_map/all_gather | solution.py:271
  1304.4 3.2 multiply_reduce_fusion.11
  1311.2 66.8 %all-reduce.35.cloned.1.call-done = (f32[8208]{0:T(1024)}, f32[8208]{0:T(1024)}) async-done(((f32[8208]{0:T(1024)}, f32[8208]{0:T(1024)}), (f32[8208]{0:T(1024)}, f32[8208]{0:T(1024)})) %all-reduce.35.cloned.1.call-update) | async-done | bytes 65680
  1387.5 66.1 %all-reduce.37.cloned.1.call-done = (f32[24592]{0:T(1024)}, f32[32784]{0:T(1024)}) async-done(((f32[24592]{0:T(1024)}, f32[32784]{0:T(1024)}), (f32[24592]{0:T(1024)}, f32[32784]{0:T(1024)})) %all-reduce.37.cloned.1.call-update) | async-done | bytes 229520
  1469.4 35.2 %all-reduce.28 = (f32[]{:T(128)}, f32[8]{0:T(128)S(1)}, f32[]{:T(128)}, f32[8]{0:T(128)S(1)}, f32[]{:T(128)}, /*index=5*/f32[]{:T(128)}, f32[8]{0:T(128)S(1)}, f...) all-reduce(f32[]{:T(128)} %get-tuple-element.230, ...), channel_id=1, replica_groups=mesh['fsdp'=8,'dp'=4] {'fsdp'}, use_global_device_ids=true, to_apply=%region_54.55 | all-reduce | flops 76 | bytes 608 | tf_op jit(solution)/shard_map/psum | solution.py:339
  1524.6 16.5 %all-gather.11 = bf16[8,1,128]{2,1,0:T(2,128)(2,1)S(1)} all-gather(bf16[1,1,128]{2,1,0:T(2,128)(2,1)S(1)} %get-tuple-element.207), channel_id=1, replica_groups=mesh['fsdp'=8,'dp'=4] {'fsdp'}, dimensions={0}, use_global_device_ids=true | all-gather | bytes 2304 | tf_op jit(solution)/shard_map/all_gather | solution.py:165
  1542.8 3.1 divide_subtract_fusion.2
  1555.5 9.7 add_convert_fusion.2
  (370 shorter events, 109.2 us)
Async XLA Ops:
  7.3 151.2 %all-gather.21.cloned.1.call-start = ((), (), s32[]{:S(2)}) async-start(), calls=%async_computation.4 | async-start | bytes 7077888 | tf_op jit(solution)/shard_map/all_gather | solution.py:156
  11.2 200.0 %all-gather.23.cloned.1.call-start = ((), (), s32[]{:S(2)}) async-start(), calls=%async_computation.5 | async-start | bytes 2359296 | tf_op jit(solution)/shard_map/all_gather | solution.py:158
  12.6 277.3 %all-gather.25.cloned.1.call-start = ((), (), s32[]{:S(2)}) async-start(), calls=%async_computation.6 | async-start | bytes 9437184 | tf_op jit(solution)/shard_map/all_gather | solution.py:162
  14.7 45.8 %copy-start.90 = (f32[128]{0:T(128)S(1)}, f32[128]{0:T(128)}, u32[]{:S(2)}) copy-start(f32[128]{0:T(128)} %param.37) | copy-start | bytes 1540
  14.8 64.6 %copy-start.94 = (f32[128]{0:T(128)S(1)}, f32[128]{0:T(128)}, u32[]{:S(2)}) copy-start(f32[128]{0:T(128)} %param.33) | copy-start | bytes 1540
  14.8 81.7 %copy-start.92 = (f32[128]{0:T(128)S(1)}, f32[128]{0:T(128)}, u32[]{:S(2)}) copy-start(f32[128]{0:T(128)} %param.32) | copy-start | bytes 1540
  14.8 142.9 %copy-start.2 = (bf16[577,1024]{1,0:T(8,128)(2,1)S(1)}, bf16[577,1024]{1,0:T(8,128)(2,1)}, u32[]{:S(2)}) copy-start(bf16[577,1024]{1,0:T(8,128)(2,1)} %param.30) | copy-start | bytes 3545092
  14.8 400.8 %all-gather.27.cloned.1.call-start = ((), (), s32[]{:S(2)}) async-start(), calls=%async_computation.7 | async-start | bytes 9437184 | tf_op jit(solution)/shard_map/all_gather | solution.py:164
  19.2 700.7 %reduce-scatter.5.cloned.1.call-start = ((), (), s32[]{:S(2)}) async-start(), calls=%async_computation.8 | async-start | bytes 12976128 | tf_op jit(solution)/shard_map/reduce_scatter | solution.py:251
  43.5 246.3 %copy-start.21 = (f32[8,1,128]{2,1,0:T(1,128)}, f32[8,1,128]{2,1,0:T(1,128)S(1)}, u32[]{:S(2)}) copy-start(f32[8,1,128]{2,1,0:T(1,128)S(1)} %convert_element_type.176) | copy-start | bytes 12292
  96.5 69.1 %copy-start.49 = (f32[8,1,128]{2,1,0:T(1,128)}, f32[8,1,128]{2,1,0:T(1,128)S(1)}, u32[]{:S(2)}) copy-start(f32[8,1,128]{2,1,0:T(1,128)S(1)} %convert_element_type.172) | copy-start | bytes 12292
  115.1 50.5 %copy-start.30 = (f32[8,1,128]{2,1,0:T(1,128)}, f32[8,1,128]{2,1,0:T(1,128)S(1)}, u32[]{:S(2)}) copy-start(f32[8,1,128]{2,1,0:T(1,128)S(1)} %convert_element_type.171) | copy-start | bytes 12292
  566.3 338.1 %reduce-scatter.11.cloned.1.call-start = ((), (), s32[]{:S(2)}) async-start(), calls=%async_computation.13 | async-start | bytes 17301504 | tf_op jit(solution)/shard_map/reduce_scatter | solution.py:259
  590.5 502.8 %reduce-scatter.9.cloned.1.call-start = ((), (), s32[]{:S(2)}) async-start(), calls=%async_computation.11 | async-start | bytes 17301504 | tf_op jit(solution)/shard_map/reduce_scatter | solution.py:257
  604.5 634.3 %reduce-scatter.7.cloned.1.call-start = ((), (), s32[]{:S(2)}) async-start(), calls=%async_computation.10 | async-start | bytes 4325376 | tf_op jit(solution)/shard_map/reduce_scatter | solution.py:253
  610.1 110.0 %copy-start.99 = (u32[32]{0:T(128)S(1)}, u32[32]{0:T(128)}, u32[]{:S(2)}) copy-start(u32[32]{0:T(128)} %constant.285) | copy-start | bytes 388
  610.1 112.5 %copy-start.98 = (u32[32]{0:T(128)S(1)}, u32[32]{0:T(128)}, u32[]{:S(2)}) copy-start(u32[32]{0:T(128)} %constant.250) | copy-start | bytes 388
  610.1 114.4 %copy-start.74 = (f32[128]{0:T(128)S(1)}, f32[128]{0:T(128)}, u32[]{:S(2)}) copy-start(f32[128]{0:T(128)} %param.43) | copy-start | bytes 1540
  610.1 645.9 %all-gather.29.cloned.1.call-start = ((), (), s32[]{:S(2)}) async-start(), calls=%async_computation.9 | async-start | bytes 1966080 | tf_op jit(solution)/shard_map/all_gather | solution.py:265
  720.0 560.2 %all-gather.33.cloned.1.call-start = ((), (), s32[]{:S(2)}) async-start(), calls=%async_computation.14 | async-start | bytes 2621440 | tf_op jit(solution)/shard_map/all_gather | solution.py:273
  733.5 170.9 %copy-start.81 = (f32[8]{0:T(128)}, f32[8]{0:T(128)S(1)}, u32[]{:S(2)}) copy-start(f32[8]{0:T(128)S(1)} %dynamic-update-slice.15) | copy-start | bytes 100
  734.9 178.5 %copy-start.82 = (f32[8]{0:T(128)}, f32[8]{0:T(128)S(1)}, u32[]{:S(2)}) copy-start(f32[8]{0:T(128)S(1)} %dynamic-update-slice.16) | copy-start | bytes 100
  736.3 168.0 %copy-start.75 = (f32[8]{0:T(128)}, f32[8]{0:T(128)S(1)}, u32[]{:S(2)}) copy-start(f32[8]{0:T(128)S(1)} %dynamic-update-slice.17) | copy-start | bytes 100
  904.4 400.0 %all-gather.31.cloned.1.call-start = ((), (), s32[]{:S(2)}) async-start(), calls=%async_computation.12 | async-start | bytes 2621440 | tf_op jit(solution)/shard_map/all_gather | solution.py:271
  915.8 188.6 %copy-start.67 = (f32[256]{0:T(256)S(1)}, f32[256]{0:T(256)}, u32[]{:S(2)}) copy-start(f32[256]{0:T(256)} %param.54) | copy-start | bytes 3076
  915.8 189.8 %copy-start.68 = (f32[128]{0:T(128)S(1)}, f32[128]{0:T(128)}, u32[]{:S(2)}) copy-start(f32[128]{0:T(128)} %param.53) | copy-start | bytes 1540
  915.8 189.8 %copy-start.69 = (f32[128]{0:T(128)S(1)}, f32[128]{0:T(128)}, u32[]{:S(2)}) copy-start(f32[128]{0:T(128)} %param.52) | copy-start | bytes 1540
  915.8 190.9 %copy-start.70 = (f32[128]{0:T(128)S(1)}, f32[128]{0:T(128)}, u32[]{:S(2)}) copy-start(f32[128]{0:T(128)} %param.56) | copy-start | bytes 1540
  915.8 190.9 %copy-start.71 = (f32[128]{0:T(128)S(1)}, f32[128]{0:T(128)}, u32[]{:S(2)}) copy-start(f32[128]{0:T(128)} %param.55) | copy-start | bytes 1540
  915.8 192.0 %copy-start.72 = (f32[128]{0:T(128)S(1)}, f32[128]{0:T(128)}, u32[]{:S(2)}) copy-start(f32[128]{0:T(128)} %param.59) | copy-start | bytes 1540
  915.8 192.0 %copy-start.73 = (f32[128]{0:T(128)S(1)}, f32[128]{0:T(128)}, u32[]{:S(2)}) copy-start(f32[128]{0:T(128)} %param.57) | copy-start | bytes 1540
  915.8 193.2 %copy-start.55 = (f32[512]{0:T(512)S(1)}, f32[512]{0:T(512)}, u32[]{:S(2)}) copy-start(f32[512]{0:T(512)} %param.58) | copy-start | bytes 6148
  918.0 327.7 %copy-start.83 = (f32[128]{0:T(128)S(1)}, f32[128]{0:T(128)}, u32[]{:S(2)}) copy-start(f32[128]{0:T(128)} %param.46) | copy-start | bytes 1540
  1093.4 284.7 %all-reduce.35.cloned.1.call-start = ((), (), s32[]{:S(2)}) async-start(), calls=%async_computation.15 | async-start | bytes 147456
  1110.3 148.6 %copy-start.84 = (f32[128]{0:T(128)S(1)}, f32[128]{0:T(128)}, u32[]{:S(2)}) copy-start(f32[128]{0:T(128)} %param.44) | copy-start | bytes 1540
  1245.7 295.5 %copy-start.15 = (f32[128,1024]{1,0:T(8,128)}, f32[128,1024]{1,0:T(8,128)S(1)}, u32[]{:S(2)}) copy-start(f32[128,1024]{1,0:T(8,128)S(1)} %get-tuple-element.164) | copy-start | bytes 1572868
  1246.3 140.3 %copy-start.45 = (f32[128]{0:T(128)}, f32[128]{0:T(128)S(1)}, u32[]{:S(2)}) copy-start(f32[128]{0:T(128)S(1)} %get-tuple-element.163) | copy-start | bytes 1540
  1261.7 45.9 %copy-start.20 = (f32[24592]{0:T(1024)}, f32[24592]{0:T(1024)S(1)}, u32[]{:S(2)}) copy-start(f32[24592]{0:T(1024)S(1)} %dynamic-update-slice.7) | copy-start | bytes 295108
  1284.0 263.9 %copy-start.38 = (f32[512]{0:T(512)}, f32[512]{0:T(512)S(1)}, u32[]{:S(2)}) copy-start(f32[512]{0:T(512)S(1)} %get-tuple-element.160) | copy-start | bytes 6148
  1286.3 94.8 %copy-start.53 = (f32[1024]{0:T(1024)S(1)}, f32[1024]{0:T(1024)}, u32[]{:S(2)}) copy-start(f32[1024]{0:T(1024)} %param.51) | copy-start | bytes 12292
  1286.3 94.8 %copy-start.54 = (f32[1024]{0:T(1024)S(1)}, f32[1024]{0:T(1024)}, u32[]{:S(2)}) copy-start(f32[1024]{0:T(1024)} %param.47) | copy-start | bytes 12292
  1286.3 167.3 %all-reduce.37.cloned.1.call-start = ((), (), s32[]{:S(2)}) async-start(), calls=%async_computation.16 | async-start | bytes 475136
  1381.1 160.0 %copy-start.34 = (f32[1024]{0:T(1024)}, f32[1024]{0:T(1024)S(1)}, u32[]{:S(2)}) copy-start(f32[1024]{0:T(1024)S(1)} %get-tuple-element.234) | copy-start | bytes 12292
  1381.1 166.8 %copy-start.37 = (f32[1024]{0:T(1024)}, f32[1024]{0:T(1024)S(1)}, u32[]{:S(2)}) copy-start(f32[1024]{0:T(1024)S(1)} %get-tuple-element.233) | copy-start | bytes 12292
  1453.6 87.5 %copy-start.17 = (f32[128,1024]{1,0:T(8,128)S(1)}, f32[128,1024]{1,0:T(8,128)}, u32[]{:S(2)}) copy-start(f32[128,1024]{1,0:T(8,128)} %param.36) | copy-start | bytes 1572868
  1458.8 84.0 %copy-start.27 = (f32[3072]{0:T(1024)}, f32[3072]{0:T(1024)S(1)}, u32[]{:S(2)}) copy-start(f32[3072]{0:T(1024)S(1)} %fusion.63) | copy-start | bytes 36868
  1464.0 81.9 %copy-start.24 = (f32[4096]{0:T(1024)}, f32[4096]{0:T(1024)S(1)}, u32[]{:S(2)}) copy-start(f32[4096]{0:T(1024)S(1)} %fusion.62) | copy-start | bytes 49156
  1464.1 78.8 %copy-start.44 = (f32[128]{0:T(128)S(1)}, f32[128]{0:T(128)}, u32[]{:S(2)}) copy-start(f32[128]{0:T(128)} %get-tuple-element.169) | copy-start | bytes 1540
  (65 other events, 544.6 us)
Sparse Core Ops, SparseCore 0:
  11.3 101.9 all-gather.20
  116.0 47.6 all-gather.22
  166.4 123.4 all-gather.24
  292.4 123.0 all-gather.26
  566.4 153.5 reduce-scatter.4
  722.2 182.1 reduce-scatter.10
  906.8 186.5 reduce-scatter.8
  1095.7 143.0 reduce-scatter.6
  1240.4 15.5 all-gather.28
  1257.5 22.5 all-gather.32
  1281.8 22.5 all-gather.30
  1309.3 68.6 all-reduce.34
  1383.0 70.6 all-reduce.36
